TPU v7x, 256 devices: a whole 4x4x8 slice. The times are simulated.
256 devices in a mesh: dp: 8 (over y, core), space: 32 (over z, x).
Axes of the slice: x: 4, y: 4, z: 8, core: 2. Of those that a mesh axis runs over, the one named last changes fastest.
Arguments:
- features: bfloat16 [8, 1024, 64, 512], P('dp', 'space'), may hold values from -50 to 50
- owners: int32 [8, 1024, 1], P('dp', 'space'), may hold values from 0 to 31; in each aligned block of 32 rows (0 to 31, 32 to 63, ..., all dimensions but the last counted through in order) at most 2 rows name the same one
- neighbors: int32 [8, 1024, 3], P('dp', 'space'), may hold values from -1 to 1022, as said below
- w_reduce: bfloat16 [512, 128], replicated, may hold values from -0.25 to 0.25
- w_spatial: bfloat16 [1152, 128], replicated, may hold values from -0.1875 to 0.1875
- w_expand: bfloat16 [128, 512], replicated, may hold values from -0.5 to 0.5
- w_short: bfloat16 [512, 512], replicated, may hold values from -0.25 to 0.25
- gains_mid: float32 [2, 128], replicated, may hold values from 0.25 to 1.75
- shifts_mid: float32 [2, 128], replicated, may hold values from -2.5 to 2.5
- gains_wide: float32 [2, 512], replicated, may hold values from 0.25 to 1.75
- shifts_wide: float32 [2, 512], replicated, may hold values from -2.5 to 2.5
- cotangent: bfloat16 [8, 2048, 16, 512], P('dp', 'space'), may hold values from -6 to 6
Outputs:
- block_out: bfloat16 [8, 2048, 16, 512], P('dp', 'space')
- grad_features: bfloat16 [8, 1024, 64, 512], P('dp', 'space')
- grad_reduce: float32 [512, 128], P('space')
- grad_spatial: float32 [1152, 128], P('space')
- grad_expand: float32 [128, 512], P('space')
- grad_short: float32 [512, 512], P('space')
- grad_gains_mid: float32 [2, 128], P(None, 'space')
- grad_shifts_mid: float32 [2, 128], P(None, 'space')
- grad_gains_wide: float32 [2, 512], P(None, 'space')
- grad_shifts_wide: float32 [2, 512], P(None, 'space')
Inputs may be any that keep to these rules, and one draw needn't show every extreme that they name: `owners`: among the 32 tiles of one block no owner is named more than 2 times. `neighbors`: entries are tile indices of the same slide or -1 for none; for tile t every index lies between t - 32 and t - 1.
All inputs are finite; a program needn't handle non-finite values.
Results may differ from a plain program's by a relative error of at most 0.02.
Values may be sent and summed in bfloat16 or wider, within the bound.
No kernel may reach another device: no remote copies, remote signals or barrier semaphores. Data moves between devices by JAX's collectives and lax.ppermute only.
A program may use at most 64 MiB of HBM per device.

v0:
```python
import math
import jax
import jax.numpy as jnp
from jax import lax
from jax.sharding import PartitionSpec as P

GROUPS = 32
SIDE = 8
EPS = 1e-05


def passed_along(shard, axis, by):
    peers = lax.axis_size(axis)
    pairs = [(i, i + by) for i in range(peers) if 0 <= i + by < peers]
    return lax.ppermute(shard, axis, pairs)


def smooth(values):
    return values * jax.nn.sigmoid(values)


def smooth_slope(values):
    sig = jax.nn.sigmoid(values)
    return sig * (1.0 + values * (1.0 - sig))


def group_total(per_channel):
    width = per_channel.shape[-1]
    grouped = per_channel.reshape(per_channel.shape[:-1] + (GROUPS, width // GROUPS))
    return jnp.repeat(jnp.sum(grouped, axis=-1), width // GROUPS, axis=-1)


def moments(conv_out):
    values = conv_out.astype(jnp.float32)
    return jnp.stack([jnp.sum(values, axis=0), jnp.sum(values * values, axis=0)])


def grad_moments(upstream, normed):
    return jnp.stack([jnp.sum(upstream, axis=0), jnp.sum(upstream * normed, axis=0)])


def norm_forward(conv_out, totals, members, gain_row, shift_row):
    center = group_total(totals[0]) / members
    spread = group_total(totals[1]) / members - center * center
    inv_spread = lax.rsqrt(spread + EPS)
    normed = (conv_out.astype(jnp.float32) - center) * inv_spread
    return (normed, normed * gain_row + shift_row, center, inv_spread)


def norm_backward(upstream, normed, inv_spread, gain_row, totals, members):
    first = group_total(gain_row * totals[0]) / members
    second = group_total(gain_row * totals[1]) / members
    return inv_spread * (gain_row * upstream - first - normed * second)


def slide_total(partial_sums):
    return lax.psum(partial_sums, "space")


def body(
    features,
    owners,
    neighbors,
    w_reduce,
    w_spatial,
    w_expand,
    w_short,
    gains_mid,
    shifts_mid,
    gains_wide,
    shifts_wide,
    cotangent,
):
    spaces = lax.axis_size("space")
    my_index = lax.axis_index("space")
    tile_count = features.shape[1]
    positions = SIDE * SIDE
    half = SIDE // 2
    quarter = half * half
    width_in = features.shape[3]
    width_mid = w_reduce.shape[1]
    tiles_total = tile_count * spaces
    slide_count = features.shape[0] * lax.axis_size("dp")
    capacity = cotangent.shape[1] // spaces
    members_in = tiles_total * positions * (width_mid // GROUPS)
    members_mid = tiles_total * quarter * (width_mid // GROUPS)
    members_wide = tiles_total * quarter * (width_in // GROUPS)
    row_width = SIDE * width_mid
    cot_owned = cotangent[0].reshape(spaces, capacity, quarter * width_in)
    cot_home = lax.all_to_all(cot_owned, "space", split_axis=0, concat_axis=0, tiled=True)
    flat_in = features[0].reshape(tile_count * positions, width_in)
    conv_one = jnp.dot(flat_in, w_reduce, preferred_element_type=jnp.float32).astype(jnp.bfloat16)
    totals_one = slide_total(moments(conv_one))
    normed_one, pre_one, center_one, scale_one = norm_forward(
        conv_one, totals_one, members_in, gains_mid[0], shifts_mid[0]
    )
    act_one = smooth(pre_one).astype(jnp.bfloat16)
    grid_source = act_one.reshape(tile_count, SIDE, SIDE, width_mid)
    own_rims = jnp.concatenate(
        [grid_source[:, SIDE - 1], grid_source[:, :, SIDE - 1]], axis=1
    ).reshape(tile_count, 2 * row_width)
    prior_rims = passed_along(own_rims, "space", 1)
    rim_pool = jnp.concatenate([prior_rims, own_rims], axis=0)
    links = neighbors[0]
    first_index = (my_index - 1) * tile_count
    pool_slots = jnp.arange(2 * tile_count, dtype=jnp.int32)

    def pick_matrix(column):
        target = links[:, column]
        return (target[:, None] - first_index == pool_slots[None, :]) & (target[:, None] >= 0)

    match_top = pick_matrix(0)
    match_left = pick_matrix(1)
    match_corner = pick_matrix(2)
    top_row = (
        jnp.dot(
            match_top.astype(jnp.bfloat16),
            rim_pool[:, :row_width],
            preferred_element_type=jnp.float32,
        )
        .astype(jnp.bfloat16)
        .reshape(tile_count, SIDE, width_mid)
    )
    left_col = (
        jnp.dot(
            match_left.astype(jnp.bfloat16),
            rim_pool[:, row_width:],
            preferred_element_type=jnp.float32,
        )
        .astype(jnp.bfloat16)
        .reshape(tile_count, SIDE, width_mid)
    )
    corner_cell = jnp.dot(
        match_corner.astype(jnp.bfloat16),
        rim_pool[:, row_width - width_mid : row_width],
        preferred_element_type=jnp.float32,
    ).astype(jnp.bfloat16)
    grid_act = act_one.reshape(tile_count, SIDE, SIDE, width_mid)
    first_line = jnp.concatenate([corner_cell[:, None], top_row], axis=1)
    lower_rows = jnp.concatenate([left_col[:, :, None], grid_act], axis=2)
    padded = jnp.concatenate([first_line[:, None], lower_rows], axis=1)
    columns = jnp.concatenate(
        [
            padded[
                :, offset_row : offset_row + SIDE - 1 : 2, offset_col : offset_col + SIDE - 1 : 2
            ]
            for offset_row in range(3)
            for offset_col in range(3)
        ],
        axis=-1,
    ).reshape(tile_count * quarter, 9 * width_mid)
    conv_two = jnp.dot(columns, w_spatial, preferred_element_type=jnp.float32).astype(jnp.bfloat16)
    totals_two = slide_total(moments(conv_two))
    normed_two, pre_two, center_two, scale_two = norm_forward(
        conv_two, totals_two, members_mid, gains_mid[1], shifts_mid[1]
    )
    act_two = smooth(pre_two).astype(jnp.bfloat16)
    conv_three = jnp.dot(act_two, w_expand, preferred_element_type=jnp.float32).astype(jnp.bfloat16)
    sub_in = (
        features[0]
        .reshape(tile_count, SIDE, SIDE, width_in)[:, ::2, ::2]
        .reshape(tile_count * quarter, width_in)
    )
    conv_short = jnp.dot(sub_in, w_short, preferred_element_type=jnp.float32).astype(jnp.bfloat16)
    totals_wide = slide_total(jnp.concatenate([moments(conv_three), moments(conv_short)], axis=0))
    normed_three, pre_three, center_three, scale_three = norm_forward(
        conv_three, totals_wide[:2], members_wide, gains_wide[0], shifts_wide[0]
    )
    normed_short, pre_short, center_short, scale_short = norm_forward(
        conv_short, totals_wide[2:], members_wide, gains_wide[1], shifts_wide[1]
    )
    summed = pre_three + pre_short
    result = smooth(summed).astype(jnp.bfloat16)
    owner_of = owners[0][:, 0]
    owner_hits = (owner_of[:, None] == jnp.arange(spaces, dtype=jnp.int32)[None, :]).astype(
        jnp.int32
    )
    before = jnp.cumsum(owner_hits, axis=0) - owner_hits
    rank_in = jnp.sum(before * owner_hits, axis=1)
    slot_of = owner_of * capacity + rank_in
    dispatch = (jnp.arange(spaces * capacity, dtype=jnp.int32)[:, None] == slot_of[None, :]).astype(
        jnp.bfloat16
    )
    outgoing = (
        jnp.dot(
            dispatch,
            result.reshape(tile_count, quarter * width_in),
            preferred_element_type=jnp.float32,
        )
        .astype(jnp.bfloat16)
        .reshape(spaces, capacity, quarter * width_in)
    )
    arrived = lax.all_to_all(outgoing, "space", split_axis=0, concat_axis=0, tiled=True)
    block_out = arrived.reshape(1, spaces * capacity, quarter, width_in)
    picked = jnp.dot(
        dispatch.T,
        cot_home.reshape(spaces * capacity, quarter * width_in),
        preferred_element_type=jnp.float32,
    ).reshape(tile_count * quarter, width_in)
    upstream = picked * smooth_slope(summed)
    totals_back = slide_total(
        jnp.concatenate(
            [grad_moments(upstream, normed_three), grad_moments(upstream, normed_short)], axis=0
        )
    )
    dconv_three = norm_backward(
        upstream, normed_three, scale_three, gains_wide[0], totals_back[:2], members_wide
    ).astype(jnp.bfloat16)
    dconv_short = norm_backward(
        upstream, normed_short, scale_short, gains_wide[1], totals_back[2:], members_wide
    ).astype(jnp.bfloat16)
    grad_expand_part = jnp.dot(act_two.T, dconv_three, preferred_element_type=jnp.float32)
    grad_short_part = jnp.dot(sub_in.T, dconv_short, preferred_element_type=jnp.float32)
    back_two = jnp.dot(dconv_three, w_expand.T, preferred_element_type=jnp.float32)
    back_two = back_two * smooth_slope(pre_two)
    totals_two_back = slide_total(grad_moments(back_two, normed_two))
    dconv_two = norm_backward(
        back_two, normed_two, scale_two, gains_mid[1], totals_two_back, members_mid
    ).astype(jnp.bfloat16)
    grad_spatial_part = jnp.dot(columns.T, dconv_two, preferred_element_type=jnp.float32)
    back_cols = jnp.dot(dconv_two, w_spatial.T, preferred_element_type=jnp.float32).reshape(
        tile_count, half, half, 9, width_mid
    )
    back_pad = jnp.zeros((tile_count, SIDE + 1, SIDE + 1, width_mid), jnp.float32)
    for offset_row in range(3):
        for offset_col in range(3):
            back_pad = back_pad.at[
                :, offset_row : offset_row + SIDE - 1 : 2, offset_col : offset_col + SIDE - 1 : 2
            ].add(back_cols[:, :, :, 3 * offset_row + offset_col])
    to_top = back_pad[:, 0, 1:].reshape(tile_count, row_width)
    to_left = back_pad[:, 1:, 0].reshape(tile_count, row_width)
    to_corner = back_pad[:, 0, 0]
    rows_back = jnp.dot(match_top.astype(jnp.float32).T, to_top, precision=lax.Precision.HIGHEST)
    corner_back = jnp.dot(
        match_corner.astype(jnp.float32).T, to_corner, precision=lax.Precision.HIGHEST
    )
    rows_back = rows_back.at[:, row_width - width_mid :].add(corner_back)
    cols_back = jnp.dot(match_left.astype(jnp.float32).T, to_left, precision=lax.Precision.HIGHEST)
    rim_back = jnp.concatenate([rows_back, cols_back], axis=1)
    from_next = passed_along(rim_back[:tile_count].astype(jnp.bfloat16), "space", -1).astype(
        jnp.float32
    )
    own_back = (rim_back[tile_count:] + from_next).reshape(tile_count, 2 * SIDE, width_mid)
    inner = back_pad[:, 1:, 1:]
    inner = inner.at[:, SIDE - 1].add(own_back[:, :SIDE]).at[:, :, SIDE - 1].add(own_back[:, SIDE:])
    back_one = (inner * smooth_slope(pre_one).reshape(tile_count, SIDE, SIDE, width_mid)).reshape(
        tile_count * positions, width_mid
    )
    totals_one_back = slide_total(grad_moments(back_one, normed_one))
    dconv_one = norm_backward(
        back_one, normed_one, scale_one, gains_mid[0], totals_one_back, members_in
    ).astype(jnp.bfloat16)
    grad_reduce_part = jnp.dot(flat_in.T, dconv_one, preferred_element_type=jnp.float32)
    back_in = jnp.dot(dconv_one, w_reduce.T, preferred_element_type=jnp.float32).reshape(
        tile_count, SIDE, SIDE, width_in
    )
    back_short = jnp.dot(dconv_short, w_short.T, preferred_element_type=jnp.float32).reshape(
        tile_count, half, half, width_in
    )
    back_in = back_in.at[:, ::2, ::2].add(back_short)
    grad_features = back_in.reshape(1, tile_count, positions, width_in).astype(jnp.bfloat16)
    gain_mid_full = jnp.stack([totals_one_back[1], totals_two_back[1]])
    shift_mid_full = jnp.stack([totals_one_back[0], totals_two_back[0]])
    gain_wide_full = jnp.stack([totals_back[1], totals_back[3]])
    shift_wide_full = jnp.stack([totals_back[0], totals_back[2]])

    def own_part(array):
        share = array.shape[1] // spaces
        return lax.dynamic_slice_in_dim(array, my_index * share, share, 1)

    whole = (
        lax.psum(grad_reduce_part.astype(jnp.bfloat16), "dp").astype(jnp.float32),
        lax.psum(grad_spatial_part.astype(jnp.bfloat16), "dp").astype(jnp.float32),
        lax.psum(grad_expand_part.astype(jnp.bfloat16), "dp").astype(jnp.float32),
        lax.psum(grad_short_part.astype(jnp.bfloat16), "dp").astype(jnp.float32),
        lax.psum(gain_mid_full.astype(jnp.bfloat16), "dp").astype(jnp.float32),
        lax.psum(shift_mid_full.astype(jnp.bfloat16), "dp").astype(jnp.float32),
        lax.psum(gain_wide_full.astype(jnp.bfloat16), "dp").astype(jnp.float32),
        lax.psum(shift_wide_full.astype(jnp.bfloat16), "dp").astype(jnp.float32),
    )
    shares = (
        lax.psum_scatter(
            whole[0].astype(jnp.bfloat16), "space", scatter_dimension=0, tiled=True
        ).astype(jnp.float32),
        lax.psum_scatter(
            whole[1].astype(jnp.bfloat16), "space", scatter_dimension=0, tiled=True
        ).astype(jnp.float32),
        lax.psum_scatter(
            whole[2].astype(jnp.bfloat16), "space", scatter_dimension=0, tiled=True
        ).astype(jnp.float32),
        lax.psum_scatter(
            whole[3].astype(jnp.bfloat16), "space", scatter_dimension=0, tiled=True
        ).astype(jnp.float32),
    )
    summed_all = (
        shares[0],
        shares[1],
        shares[2],
        shares[3],
        own_part(whole[4]),
        own_part(whole[5]),
        own_part(whole[6]),
        own_part(whole[7]),
    )
    scale_in = 1.0 / math.sqrt(slide_count * tiles_total * positions)
    scale_out = 1.0 / math.sqrt(slide_count * tiles_total * quarter)
    mid_scale = jnp.array([[scale_in], [scale_out]], jnp.float32)
    return (
        block_out,
        grad_features,
        summed_all[0] * scale_in,
        summed_all[1] * scale_out,
        summed_all[2] * scale_out,
        summed_all[3] * scale_out,
        summed_all[4] * mid_scale,
        summed_all[5] * mid_scale,
        summed_all[6] * scale_out,
        summed_all[7] * scale_out,
    )


def solution(mesh):
    placed = (
        P("dp", "space", None, None),
        P("dp", "space", None),
        P("dp", "space", None),
        P(),
        P(),
        P(),
        P(),
        P(),
        P(),
        P(),
        P(),
        P("dp", "space", None, None),
    )
    return jax.shard_map(
        body,
        mesh=mesh,
        in_specs=placed,
        out_specs=(
            P("dp", "space", None, None),
            P("dp", "space", None, None),
            P("space", None),
            P("space", None),
            P("space", None),
            P("space", None),
            P(None, "space"),
            P(None, "space"),
            P(None, "space"),
            P(None, "space"),
        ),
        check_vma=False,
    )
```

profile of v0, /device:TPU:4, one launch (start us, length us, event | category | flops | bytes accessed | tf_op | source)
XLA Modules:
  0.0 1519.2 jit_solution(11342063091150273757)
XLA Ops:
  7.2 2.7 reshape_squeeze.49
  9.9 11.8 all-to-all-start.1
  21.8 2.3 fusion.86
  24.1 81.0 %psum.98 = f32[2,128]{1,0:T(2,128)S(1)} all-reduce(f32[2,128]{1,0:T(2,128)S(1)} %pad_maximum_fusion.7), channel_id=1, replica_groups=mesh['dp'=8,'space'=32] {'space'}, use_global_device_ids=true, to_apply=%region_4.0 | all-reduce | flops 256 | bytes 2048 | tf_op jit(solution)/shard_map/psum | solution.py:57
  109.0 2.9 collective-permute-start
  112.0 37.4 %slice.296 = bf16[32,4,4,128]{3,2,1,0:T(4,128)(2,1)} slice(bf16[32,8,8,128]{3,2,1,0:T(8,128)(2,1)S(1)} %bitcast.217), slice={[0:32:1], [1:8:2], [1:8:2], [0:128:1]} | slice | bytes 262144 | tf_op jit(solution)/shard_map/slice | solution.py:144
  149.4 37.3 %slice.295 = bf16[32,4,4,128]{3,2,1,0:T(4,128)(2,1)} slice(bf16[32,8,8,128]{3,2,1,0:T(8,128)(2,1)S(1)} %bitcast.218), slice={[0:32:1], [1:8:2], [0:7:2], [0:128:1]} | slice | bytes 262144 | tf_op jit(solution)/shard_map/slice | solution.py:144
  186.7 37.3 %slice.293 = bf16[32,4,4,128]{3,2,1,0:T(4,128)(2,1)} slice(bf16[32,8,8,128]{3,2,1,0:T(8,128)(2,1)S(1)} %bitcast.219), slice={[0:32:1], [0:7:2], [1:8:2], [0:128:1]} | slice | bytes 262144 | tf_op jit(solution)/shard_map/slice | solution.py:144
  224.0 37.3 %slice.292 = bf16[32,4,4,128]{3,2,1,0:T(4,128)(2,1)} slice(bf16[32,8,8,128]{3,2,1,0:T(8,128)(2,1)S(1)} %bitcast.220), slice={[0:32:1], [0:7:2], [0:7:2], [0:128:1]} | slice | bytes 262144 | tf_op jit(solution)/shard_map/slice | solution.py:144
  270.9 47.3 %slice.301 = bf16[32,4,4,512]{3,2,1,0:T(4,128)(2,1)S(1)} slice(bf16[32,8,8,512]{3,2,1,0:T(8,128)(2,1)} %bitcast.213), slice={[0:32:1], [0:8:2], [0:8:2], [0:512:1]} | slice | bytes 1048576 | tf_op jit(solution)/shard_map/slice | solution.py:160
  321.1 1.8 convert_reduce_fusion
  324.9 37.4 %slice.290 = bf16[32,4,4,128]{3,2,1,0:T(4,128)(2,1)} slice(bf16[32,9,9,128]{3,2,1,0:T(8,128)(2,1)S(1)} %maximum_maximum_fusion), slice={[0:32:1], [0:7:2], [2:9:2], [0:128:1]} | slice | bytes 262144 | tf_op jit(solution)/shard_map/slice | solution.py:144
  362.2 37.2 %slice.289 = bf16[32,4,4,128]{3,2,1,0:T(4,128)(2,1)} slice(bf16[32,9,9,128]{3,2,1,0:T(8,128)(2,1)S(1)} %maximum_maximum_fusion), slice={[0:32:1], [0:7:2], [1:8:2], [0:128:1]} | slice | bytes 262144 | tf_op jit(solution)/shard_map/slice | solution.py:144
  399.5 37.3 %slice.288 = bf16[32,4,4,128]{3,2,1,0:T(4,128)(2,1)} slice(bf16[32,9,9,128]{3,2,1,0:T(8,128)(2,1)S(1)} %maximum_maximum_fusion), slice={[0:32:1], [0:7:2], [0:7:2], [0:128:1]} | slice | bytes 262144 | tf_op jit(solution)/shard_map/slice | solution.py:144
  437.2 2.9 slice.291
  440.1 4.7 slice.294
  453.8 2.4 reshape.378
  456.8 69.6 %psum.99 = f32[2,128]{1,0:T(2,128)S(1)} all-reduce(f32[2,128]{1,0:T(2,128)S(1)} %pad_maximum_fusion.8), channel_id=1, replica_groups=mesh['dp'=8,'space'=32] {'space'}, use_global_device_ids=true, to_apply=%region_9.0 | all-reduce | flops 256 | bytes 2048 | tf_op jit(solution)/shard_map/psum | solution.py:57
  527.3 2.0 convert_reduce_fusion.1
  529.3 72.8 %psum.100 = f32[4,512]{1,0:T(4,128)S(1)} all-reduce(f32[4,512]{1,0:T(4,128)S(1)} %pad_maximum_fusion.3), channel_id=1, replica_groups=mesh['dp'=8,'space'=32] {'space'}, use_global_device_ids=true, to_apply=%region_16.0 | all-reduce | flops 2048 | bytes 16384 | tf_op jit(solution)/shard_map/psum | solution.py:57
  603.7 2.2 reshape.383
  605.9 2.6 fusion.48
  608.5 2.4 reshape.384
  610.9 3.5 fusion.15
  614.4 70.6 %psum.101 = f32[4,512]{1,0:T(4,128)S(1)} all-reduce(f32[4,512]{1,0:T(4,128)S(1)} %pad_maximum_fusion.4), channel_id=1, replica_groups=mesh['dp'=8,'space'=32] {'space'}, use_global_device_ids=true, to_apply=%region_24.25 | all-reduce | flops 2048 | bytes 16384 | tf_op jit(solution)/shard_map/psum | solution.py:57
  686.6 2.9 fusion.28
  691.3 2.2 fusion.87
  693.5 71.7 %psum.102 = f32[2,128]{1,0:T(2,128)S(1)} all-reduce(f32[2,128]{1,0:T(2,128)S(1)} %pad_maximum_fusion.9), channel_id=1, replica_groups=mesh['dp'=8,'space'=32] {'space'}, use_global_device_ids=true, to_apply=%region_29.30 | all-reduce | flops 256 | bytes 2048 | tf_op jit(solution)/shard_map/psum | solution.py:57
  768.9 73.4 %fusion = bf16[48,128]{1,0:T(8,128)(2,1)} fusion(bf16[1152,128]{1,0:T(8,128)(2,1)} %convolution_convert_fusion.1), kind=kCustom, calls=%all-reduce-scatter | all-reduce-scatter fusion | flops 196609 | bytes 308224
  843.6 6.6 collective-permute-start.8
  850.2 15.4 %collective-permute-start.7 = (bf16[48,128]{1,0:T(8,128)(2,1)}, bf16[48,128]{1,0:T(8,128)(2,1)}, u32[]{:S(2)}, u32[]{:S(2)}) collective-permute-start(bf16[48,128]{1,0:T(8,128)(2,1)} %fusion), channel_id=1, source_target_pairs={{0,6},{1,7},{2,8},{3,9},{4,10},{5,11},{6,12},{7,13},{8,14},{9,15},... | collective-permute-start | bytes 36872
  865.6 1.9 collective-permute-start.6
  867.5 6.3 collective-permute-start.5
  873.8 2.5 fusion.2
  877.7 1.9 fusion.98
  879.6 4.2 reshape.385
  883.8 9.9 fusion.90
  899.6 2.2 scatter_fusion
  901.8 2.2 scatter_fusion.1
  904.0 2.2 scatter_fusion.2
  906.2 2.2 scatter_fusion.3
  908.3 2.2 scatter_fusion.4
  910.5 2.2 scatter_fusion.5
  912.7 2.2 scatter_fusion.6
  920.5 2.0 convolution_convert_fusion
  922.5 2.5 reshape.381
  925.1 6.4 all-to-all-start
  933.1 2.6 collective-permute-start.1
  935.8 4.7 collective-permute-done.1
  940.5 4.4 collective-permute-start.9
  946.8 71.0 %psum.103 = f32[2,128]{1,0:T(2,128)S(1)} all-reduce(f32[2,128]{1,0:T(2,128)S(1)} %pad_maximum_fusion.10), channel_id=1, replica_groups=mesh['dp'=8,'space'=32] {'space'}, use_global_device_ids=true, to_apply=%region_43.44 | all-reduce | flops 256 | bytes 2048 | tf_op jit(solution)/shard_map/psum | solution.py:57
  1019.0 2.1 fusion.4
  1024.3 3.9 collective-permute-start.3
  1028.3 5.7 collective-permute-start.2
  1035.6 4.5 concatenate.99
  1040.8 4.3 copy.88
  1045.1 3.5 scatter_fusion.9
  1048.6 2.5 convert_element_type.164
  1051.2 2.5 copy.89
  1053.7 8.1 all-reduce.6.cloned.1.call-done
  1062.5 197.1 %reduce-scatter.9.cloned.1.call-done = bf16[16,128]{1,0:T(8,128)(2,1)} async-done(((bf16[512,128]{1,0:T(8,128)(2,1)}), bf16[16,128]{1,0:T(8,128)(2,1)}) %reduce-scatter.9.cloned.1.call-update) | async-done | bytes 4112
  1260.4 218.2 %reduce-scatter.11.cloned.1.call-done = bf16[16,512]{1,0:T(8,128)(2,1)} async-done(((bf16[512,512]{1,0:T(8,128)(2,1)}), bf16[16,512]{1,0:T(8,128)(2,1)}) %reduce-scatter.11.cloned.1.call-update) | async-done | bytes 16400
  1479.5 25.6 %all-reduce.3 = (bf16[16,128]{0,1:T(8,128)(2,1)S(1)}, bf16[36,128]{1,0:T(8,128)(2,1)S(1)}, bf16[4,512]{1,0:T(4,128)(2,1)S(1)}, bf16[16,512]{0,1:T(8,128)(2,1)S(1...) all-reduce(bf16[16,128]{0,1:T(8,128)(2,1)S(1)} %copy.93, ...), channel_id=1, replica_groups=mesh['dp'=8,'space'=32] {'dp'}, use_global_device_ids=true, to_apply=%region_49.50 | all-reduce | flops 19456 | bytes 77824 | tf_op jit(solution)/shard_map/psum | solution.py:272
  1509.7 2.6 reshape.382
  (370 shorter events, 67.1 us)
Async XLA Ops:
  7.2 313.9 %copy-start = (bf16[512,512]{1,0:T(8,128)(2,1)S(1)}, bf16[512,512]{1,0:T(8,128)(2,1)}, u32[]{:S(2)}) copy-start(bf16[512,512]{1,0:T(8,128)(2,1)} %param.25) | copy-start | bytes 1572868
  9.9 11.8 copy-start.10
  9.9 593.8 %all-to-all-start.1 = ((bf16[32,2,8192]{2,1,0:T(2,128)(2,1)}), bf16[32,2,8192]{2,1,0:T(2,128)(2,1)}, u32[]{:S(2)}, u32[]{:S(2)}) async-start(bf16[32,2,8192]{2,1,0:T(2,128)(2,1)} %reshape_squeeze.49), calls=%async_computation.1 | async-start | bytes 2097152 | tf_op jit(solution)/shard_map/all_to_all | solution.py:90
  21.7 1040.1 %all-reduce.6.cloned.1.call-start = ((), (), s32[]{:S(2)}) async-start(), calls=%async_computation.6 | async-start | bytes 262144
  21.7 84.2 %copy-start.47 = (f32[2,128]{1,0:T(2,128)S(1)}, f32[2,128]{1,0:T(2,128)}, u32[]{:S(2)}) copy-start(f32[2,128]{1,0:T(2,128)} %param.26) | copy-start | bytes 3076
  21.7 84.2 %copy-start.58 = (f32[2,128]{1,0:T(2,128)S(1)}, f32[2,128]{1,0:T(2,128)}, u32[]{:S(2)}) copy-start(f32[2,128]{1,0:T(2,128)} %param.27) | copy-start | bytes 3076
  108.0 154.0 %copy-start.57 = (s32[1,32,3]{1,0,2:T(1,128)S(1)}, s32[1,32,3]{1,0,2:T(1,128)}, u32[]{:S(2)}) copy-start(s32[1,32,3]{1,0,2:T(1,128)} %param.21) | copy-start | bytes 1156
  108.0 155.1 %copy-start.46 = (f32[2,512]{1,0:T(2,128)S(1)}, f32[2,512]{1,0:T(2,128)}, u32[]{:S(2)}) copy-start(f32[2,512]{1,0:T(2,128)} %param.29) | copy-start | bytes 12292
  108.0 155.7 %copy-start.25 = (f32[2,512]{1,0:T(2,128)S(1)}, f32[2,512]{1,0:T(2,128)}, u32[]{:S(2)}) copy-start(f32[2,512]{1,0:T(2,128)} %param.28) | copy-start | bytes 12292
  108.0 162.1 %copy-start.51 = (s32[1,32,1]{1,2,0:T(1,128)S(1)}, s32[1,32,1]{1,2,0:T(1,128)}, u32[]{:S(2)}) copy-start(s32[1,32,1]{1,2,0:T(1,128)} %param.20) | copy-start | bytes 388
  109.0 214.6 %collective-permute-start = (bf16[32,2048]{1,0:T(8,128)(2,1)}, bf16[32,2048]{1,0:T(8,128)(2,1)S(1)}, u32[]{:S(2)}, u32[]{:S(2)}) collective-permute-start(bf16[32,2048]{1,0:T(8,128)(2,1)} %bitcast.208), channel_id=1, source_target_pairs={{0,1},{1,2},{2,3},{3,4},{4,5},{5,6},{6,7},{7,8},{8,9},{9,10},{10,1... | collective-permute-start | bytes 393224 | tf_op jit(solution)/shard_map/ppermute | solution.py:15
  318.3 5.2 copy-start.11
  318.3 4.6 copy-start.52
  318.4 4.6 copy-start.62
  437.1 13.2 copy-start.16
  437.2 13.9 copy-start.15
  437.2 15.3 %copy-start.14 = (bf16[32,4,4,128]{3,2,1,0:T(4,128)(2,1)S(1)}, bf16[32,4,4,128]{3,2,1,0:T(4,128)(2,1)}, u32[]{:S(2)}) copy-start(bf16[32,4,4,128]{3,2,1,0:T(4,128)(2,1)} %slice.295) | copy-start | bytes 393220
  437.2 16.0 %copy-start.13 = (bf16[32,4,4,128]{3,2,1,0:T(4,128)(2,1)S(1)}, bf16[32,4,4,128]{3,2,1,0:T(4,128)(2,1)}, u32[]{:S(2)}) copy-start(bf16[32,4,4,128]{3,2,1,0:T(4,128)(2,1)} %slice.296) | copy-start | bytes 393220
  453.1 3.1 copy-start.6
  456.2 71.0 %copy-start.55 = (f32[128]{0:T(128)S(1)}, f32[128]{0:T(128)}, u32[]{:S(2)}) copy-start(f32[128]{0:T(128)} %get-tuple-element.173) | copy-start | bytes 1540
  456.2 71.0 %copy-start.65 = (f32[128]{0:T(128)S(1)}, f32[128]{0:T(128)}, u32[]{:S(2)}) copy-start(f32[128]{0:T(128)} %get-tuple-element.163) | copy-start | bytes 1540
  456.7 146.0 %copy-start.8 = (f32[512,128]{1,0:T(8,128)}, f32[512,128]{1,0:T(8,128)S(1)}, u32[]{:S(2)}) copy-start(f32[512,128]{1,0:T(8,128)S(1)} %get-tuple-element.168) | copy-start | bytes 786436
  456.8 72.6 %copy-start.53 = (f32[512]{0:T(512)S(1)}, f32[512]{0:T(512)}, u32[]{:S(2)}) copy-start(f32[512]{0:T(512)} %get-tuple-element.83) | copy-start | bytes 6148
  456.8 72.5 %copy-start.54 = (f32[512]{0:T(512)S(1)}, f32[512]{0:T(512)}, u32[]{:S(2)}) copy-start(f32[512]{0:T(512)} %get-tuple-element.84) | copy-start | bytes 6148
  527.3 164.1 %copy-start.67 = (f32[128]{0:T(128)}, f32[128]{0:T(128)S(1)}, u32[]{:S(2)}) copy-start(f32[128]{0:T(128)S(1)} %add_rsqrt_fusion.2) | copy-start | bytes 1540
  529.3 76.6 %copy-start.50 = (s32[32]{0:T(128)S(1)}, s32[32]{0:T(128)}, u32[]{:S(2)}) copy-start(s32[32]{0:T(128)} %multiply_add_fusion.2) | copy-start | bytes 388
  610.9 74.1 %copy-start.26 = (f32[2,512]{1,0:T(2,128)S(1)}, f32[2,512]{1,0:T(2,128)}, u32[]{:S(2)}) copy-start(f32[2,512]{1,0:T(2,128)} %param.28) | copy-start | bytes 12292
  685.1 4.5 copy-start.21
  686.6 3.8 copy-start.9
  686.6 3.8 copy-start.56
  686.6 3.8 copy-start.66
  691.3 73.9 %copy-start.48 = (f32[2,128]{1,0:T(2,128)S(1)}, f32[2,128]{1,0:T(2,128)}, u32[]{:S(2)}) copy-start(f32[2,128]{1,0:T(2,128)} %param.26) | copy-start | bytes 3076
  768.9 107.3 %copy-start.5 = (bf16[512,512]{1,0:T(8,128)(2,1)S(1)}, bf16[512,512]{1,0:T(8,128)(2,1)}, u32[]{:S(2)}) copy-start(bf16[512,512]{1,0:T(8,128)(2,1)} %get-tuple-element.128) | copy-start | bytes 1572868
  843.6 180.7 %collective-permute-start.8 = (bf16[48,128]{1,0:T(8,128)(2,1)}, bf16[48,128]{1,0:T(8,128)(2,1)}, u32[]{:S(2)}, u32[]{:S(2)}) collective-permute-start(bf16[48,128]{1,0:T(8,128)(2,1)} %fusion), channel_id=1, source_target_pairs={{0,7},{1,8},{2,9},{3,10},{4,11},{5,12},{6,13},{7,14},{8,15},{9,16}... | collective-permute-start | bytes 36872
  850.2 178.1 %collective-permute-start.7 = (bf16[48,128]{1,0:T(8,128)(2,1)}, bf16[48,128]{1,0:T(8,128)(2,1)}, u32[]{:S(2)}, u32[]{:S(2)}) collective-permute-start(bf16[48,128]{1,0:T(8,128)(2,1)} %fusion), channel_id=1, source_target_pairs={{0,6},{1,7},{2,8},{3,9},{4,10},{5,11},{6,12},{7,13},{8,14},{9,15},... | collective-permute-start | bytes 36872
  865.6 169.3 %collective-permute-start.6 = (bf16[48,128]{1,0:T(8,128)(2,1)}, bf16[48,128]{1,0:T(8,128)(2,1)}, u32[]{:S(2)}, u32[]{:S(2)}) collective-permute-start(bf16[48,128]{1,0:T(8,128)(2,1)} %fusion), channel_id=1, source_target_pairs={{0,5},{1,6},{2,7},{3,8},{4,9},{5,10},{6,11},{7,12},{8,13},{9,14},{... | collective-permute-start | bytes 36872
  867.5 167.5 %collective-permute-start.5 = (bf16[48,128]{1,0:T(8,128)(2,1)}, bf16[48,128]{1,0:T(8,128)(2,1)}, u32[]{:S(2)}, u32[]{:S(2)}) collective-permute-start(bf16[48,128]{1,0:T(8,128)(2,1)} %fusion), channel_id=1, source_target_pairs={{0,4},{1,5},{2,6},{3,7},{4,8},{5,9},{6,10},{7,11},{8,12},{9,13},{1... | collective-permute-start | bytes 36872
  925.1 6.7 copy-start.18
  925.1 6.8 copy-start.39
  925.1 6.8 copy-start.43
  925.1 7.2 copy-start.17
  925.1 7.3 copy-start.37
  925.1 7.3 copy-start.41
  925.1 7.7 copy-start.61
  925.1 7.7 copy-start.64
  925.1 584.6 %all-to-all-start = ((bf16[32,2,8192]{2,1,0:T(2,128)(2,1)}), bf16[32,2,8192]{2,1,0:T(2,128)(2,1)}, u32[]{:S(2)}, u32[]{:S(2)}) async-start(bf16[32,2,8192]{2,1,0:T(2,128)(2,1)} %reshape.381), calls=%async_computation | async-start | bytes 2097152 | tf_op jit(solution)/shard_map/all_to_all | solution.py:193
  931.5 4.2 copy-start.22
  931.5 9.0 copy-start.27
  931.5 328.1 %reduce-scatter.9.cloned.1.call-start = ((), (), s32[]{:S(2)}) async-start(), calls=%async_computation.4 | async-start | bytes 135168
  933.1 11.9 copy-start.2
  933.1 7.3 collective-permute-start.1
  935.8 9.4 copy-start.3
  940.5 82.5 %collective-permute-start.9 = (bf16[36,128]{1,0:T(8,128)(2,1)S(1)}, bf16[36,128]{1,0:T(8,128)(2,1)S(1)}, u32[]{:S(2)}, u32[]{:S(2)}) collective-permute-start(bf16[36,128]{1,0:T(8,128)(2,1)S(1)} %copy-done.27), channel_id=1, source_target_pairs={{0,8},{1,9},{2,10},{3,11},{4,12},{5,13},{6,14},{7,15},{8,16},{9,17... | collective-permute-start | bytes 27656
  946.5 71.3 %copy-start.49 = (f32[2,128]{1,0:T(2,128)S(1)}, f32[2,128]{1,0:T(2,128)}, u32[]{:S(2)}) copy-start(f32[2,128]{1,0:T(2,128)} %param.26) | copy-start | bytes 3076
  946.5 72.2 %copy-start.45 = (f32[128]{0:T(128)S(1)}, f32[128]{0:T(128)}, u32[]{:S(2)}) copy-start(f32[128]{0:T(128)} %copy-done.44) | copy-start | bytes 1540
  1018.9 3.0 copy-start.12
  1021.1 12.9 copy-start.4
  1021.9 456.8 %reduce-scatter.11.cloned.1.call-start = ((), (), s32[]{:S(2)}) async-start(), calls=%async_computation.5 | async-start | bytes 540672
  1023.0 12.0 collective-permute-start.4
  1024.3 10.7 collective-permute-start.3
  1028.3 7.3 collective-permute-start.2
  1040.8 4.3 copy-start.20
  1051.2 456.7 %copy-start.59 = (f32[2]{0:T(128)S(1)}, f32[2]{0:T(128)}, u32[]{:S(2)}) copy-start(f32[2]{0:T(128)} %constant.157) | copy-start | bytes 28
  1505.8 6.4 copy-start.1
  (19 other events, 38.7 us)
Sparse Core Ops, SparseCore 0:
  920.4 141.3 all-reduce.5
  1065.4 194.1 reduce-scatter.8
  1264.0 214.5 reduce-scatter.10
where the time goes:
time: 1530 us; the launch traced here: 1520 us
  blocking collectives  536 us (35%)
  waiting for transfers between devices  429 us (28%)
  local copies, waits for them, and re-layouts  399 us (26%)
  starting transfers between devices  69.4 us (5%)
  other arithmetic  43.4 us (3%)
  matrix products  25.9 us (2%)
  between operations  17.1 us (1%)
    psum x6, blocking collectives, slide_total(): return lax.psum(partial_sums, 'space')  437 us
    unnamed x14, waiting for transfers between devices  424 us
    slice x9, local copies, waits for them, and re-layouts, body(): padded[:, offset_row:offset_row + SIDE - 1:2, offset_col:offset_col + SID...  269 us
    unnamed x1, blocking collectives  73.4 us
    slice x1, local copies, waits for them, and re-layouts, body(): features[0].reshape(tile_count, SIDE, SIDE, width_in)[:, ::2, ::2]  47.3 us
    unnamed x11, starting transfers between devices  45.8 us
  transfers between devices with their start and end apart: 15, of which 5 were waited for; matrix products, arithmetic and copies ran while one was open for 29% of the time, Pallas kernels for 0%

commit v1 on v0

--- a/solution.py
+++ b/solution.py
@@ -54,7 +54,7 @@
 
 
 def slide_total(partial_sums):
-    return lax.psum(partial_sums, "space")
+    return jnp.sum(lax.all_gather(partial_sums, "space"), axis=0)
 
 
 def body(

time: 1530 us -> 1410 us (0.922)
  blocking collectives: 536 us -> 396 us
  waiting for transfers between devices: 429 us -> 451 us
    psum x6 -> x0, blocking collectives: 437 us -> none  [slide_total(): return lax.psum(partial_sums, 'space')]
    all_gather x0 -> x6, blocking collectives: none -> 296 us  [slide_total(): return jnp.sum(lax.all_gather(partial_sums, 'space'), axis=0)]
    unnamed x14, waiting for transfers between devices: 424 us -> 446 us
  transfers between devices with their start and end apart: 15 -> 15, of which waited for: 5 -> 5; matrix products, arithmetic and copies ran while one was open for 29% -> 32% of each run, Pallas kernels for 0% -> 0%
where the time goes in v1:
time: 1410 us; the launch traced here: 1390 us
  waiting for transfers between devices  451 us (32%)
  local copies, waits for them, and re-layouts  398 us (28%)
  blocking collectives  396 us (28%)
  starting transfers between devices  59.3 us (4%)
  other arithmetic  44.6 us (3%)
  matrix products  25.9 us (2%)
  between operations  17.1 us (1%)
    unnamed x14, waiting for transfers between devices  446 us
    all_gather x6, blocking collectives, slide_total(): return jnp.sum(lax.all_gather(partial_sums, 'space'), axis=0)  296 us
    slice x9, local copies, waits for them, and re-layouts, body(): padded[:, offset_row:offset_row + SIDE - 1:2, offset_col:offset_col + SID...  269 us
    unnamed x1, blocking collectives  74.4 us
    slice x1, local copies, waits for them, and re-layouts, body(): features[0].reshape(tile_count, SIDE, SIDE, width_in)[:, ::2, ::2]  47.3 us
    unnamed x11, starting transfers between devices  33.5 us
  transfers between devices with their start and end apart: 15, of which 5 were waited for; matrix products, arithmetic and copies ran while one was open for 32% of the time, Pallas kernels for 0%

profile of v1, /device:TPU:4, one launch (start us, length us, event | category | flops | bytes accessed | tf_op | source)
XLA Modules:
  0.0 1392.4 jit_solution(15993537283965186884)
XLA Ops:
  7.2 2.7 reshape_squeeze.49
  9.9 11.8 all-to-all-start.1
  21.8 2.3 fusion.86
  24.1 55.3 %all-gather.6 = f32[32,2,128]{2,1,0:T(2,128)S(1)} all-gather(f32[1,2,128]{2,1,0:T(2,128)S(1)} %maximum_bitcast_fusion.3), channel_id=2, replica_groups=mesh['dp'=8,'space'=32] {'space'}, dimensions={0}, use_global_device_ids=true | all-gather | bytes 33792 | tf_op jit(solution)/shard_map/all_gather | solution.py:57
  83.2 4.3 collective-permute-start
  87.6 37.4 %slice.296 = bf16[32,4,4,128]{3,2,1,0:T(4,128)(2,1)} slice(bf16[32,8,8,128]{3,2,1,0:T(8,128)(2,1)S(1)} %bitcast.229), slice={[0:32:1], [1:8:2], [1:8:2], [0:128:1]} | slice | bytes 262144 | tf_op jit(solution)/shard_map/slice | solution.py:144
  125.0 37.3 %slice.295 = bf16[32,4,4,128]{3,2,1,0:T(4,128)(2,1)} slice(bf16[32,8,8,128]{3,2,1,0:T(8,128)(2,1)S(1)} %bitcast.230), slice={[0:32:1], [1:8:2], [0:7:2], [0:128:1]} | slice | bytes 262144 | tf_op jit(solution)/shard_map/slice | solution.py:144
  162.3 37.3 %slice.293 = bf16[32,4,4,128]{3,2,1,0:T(4,128)(2,1)} slice(bf16[32,8,8,128]{3,2,1,0:T(8,128)(2,1)S(1)} %bitcast.231), slice={[0:32:1], [0:7:2], [1:8:2], [0:128:1]} | slice | bytes 262144 | tf_op jit(solution)/shard_map/slice | solution.py:144
  199.7 37.3 %slice.292 = bf16[32,4,4,128]{3,2,1,0:T(4,128)(2,1)} slice(bf16[32,8,8,128]{3,2,1,0:T(8,128)(2,1)S(1)} %bitcast.232), slice={[0:32:1], [0:7:2], [0:7:2], [0:128:1]} | slice | bytes 262144 | tf_op jit(solution)/shard_map/slice | solution.py:144
  246.6 47.3 %slice.301 = bf16[32,4,4,512]{3,2,1,0:T(4,128)(2,1)S(1)} slice(bf16[32,8,8,512]{3,2,1,0:T(8,128)(2,1)} %bitcast.225), slice={[0:32:1], [0:8:2], [0:8:2], [0:512:1]} | slice | bytes 1048576 | tf_op jit(solution)/shard_map/slice | solution.py:160
  300.5 37.4 %slice.290 = bf16[32,4,4,128]{3,2,1,0:T(4,128)(2,1)} slice(bf16[32,9,9,128]{3,2,1,0:T(8,128)(2,1)S(1)} %maximum_maximum_fusion), slice={[0:32:1], [0:7:2], [2:9:2], [0:128:1]} | slice | bytes 262144 | tf_op jit(solution)/shard_map/slice | solution.py:144
  337.9 37.2 %slice.289 = bf16[32,4,4,128]{3,2,1,0:T(4,128)(2,1)} slice(bf16[32,9,9,128]{3,2,1,0:T(8,128)(2,1)S(1)} %maximum_maximum_fusion), slice={[0:32:1], [0:7:2], [1:8:2], [0:128:1]} | slice | bytes 262144 | tf_op jit(solution)/shard_map/slice | solution.py:144
  375.1 37.3 %slice.288 = bf16[32,4,4,128]{3,2,1,0:T(4,128)(2,1)} slice(bf16[32,9,9,128]{3,2,1,0:T(8,128)(2,1)S(1)} %maximum_maximum_fusion), slice={[0:32:1], [0:7:2], [0:7:2], [0:128:1]} | slice | bytes 262144 | tf_op jit(solution)/shard_map/slice | solution.py:144
  412.8 2.9 slice.291
  415.7 4.7 slice.294
  429.5 2.4 reshape.378
  432.4 40.8 %all-gather.7 = f32[32,2,128]{2,1,0:T(2,128)S(1)} all-gather(f32[1,2,128]{2,1,0:T(2,128)S(1)} %maximum_bitcast_fusion.4), channel_id=3, replica_groups=mesh['dp'=8,'space'=32] {'space'}, dimensions={0}, use_global_device_ids=true | all-gather | bytes 33792 | tf_op jit(solution)/shard_map/all_gather | solution.py:57
  474.2 2.0 convert_reduce_fusion.1
  476.2 47.6 %all-gather.8 = f32[32,4,512]{2,1,0:T(4,128)S(1)} all-gather(f32[1,4,512]{2,1,0:T(4,128)S(1)} %maximum_bitcast_fusion.1), channel_id=4, replica_groups=mesh['dp'=8,'space'=32] {'space'}, dimensions={0}, use_global_device_ids=true | all-gather | bytes 270336 | tf_op jit(solution)/shard_map/all_gather | solution.py:57
  525.4 2.2 reshape.383
  527.7 2.6 fusion.48
  530.3 2.4 reshape.384
  532.7 3.5 fusion.15
  536.2 62.9 %all-gather.9 = f32[32,4,512]{2,1,0:T(4,128)} all-gather(f32[1,4,512]{2,1,0:T(4,128)S(1)} %maximum_bitcast_fusion.2), channel_id=5, replica_groups=mesh['dp'=8,'space'=32] {'space'}, dimensions={0}, use_global_device_ids=true | all-gather | bytes 270336 | tf_op jit(solution)/shard_map/all_gather | solution.py:57
  601.7 2.9 fusion.28
  606.4 2.2 fusion.87
  608.6 41.3 %all-gather.10 = f32[32,2,128]{2,1,0:T(2,128)S(1)} all-gather(f32[1,2,128]{2,1,0:T(2,128)S(1)} %maximum_bitcast_fusion.5), channel_id=6, replica_groups=mesh['dp'=8,'space'=32] {'space'}, dimensions={0}, use_global_device_ids=true | all-gather | bytes 33792 | tf_op jit(solution)/shard_map/all_gather | solution.py:57
  653.2 74.4 %fusion = bf16[48,128]{1,0:T(8,128)(2,1)} fusion(bf16[1152,128]{1,0:T(8,128)(2,1)} %convolution_convert_fusion.1), kind=kCustom, calls=%all-reduce-scatter | all-reduce-scatter fusion | flops 196609 | bytes 308224
  728.9 1.9 collective-permute-start.8
  730.8 9.1 collective-permute-start.7
  739.8 1.9 collective-permute-start.6
  741.7 4.7 collective-permute-start.5
  746.4 2.5 fusion.2
  750.4 1.9 fusion.98
  752.3 4.2 reshape.385
  756.5 9.9 fusion.90
  772.3 2.2 scatter_fusion
  774.5 2.2 scatter_fusion.1
  776.7 2.2 scatter_fusion.2
  778.9 2.2 scatter_fusion.3
  781.0 2.2 scatter_fusion.4
  783.2 2.2 scatter_fusion.5
  785.4 2.2 scatter_fusion.6
  793.2 2.0 convolution_convert_fusion
  795.2 2.5 reshape.381
  797.8 7.2 all-to-all-start
  806.6 2.6 collective-permute-start.1
  809.3 4.7 collective-permute-done.1
  814.0 4.4 collective-permute-start.9
  820.2 48.3 %all-gather.11 = f32[32,2,128]{2,1,0:T(2,128)S(1)} all-gather(f32[1,2,128]{2,1,0:T(2,128)S(1)} %maximum_bitcast_fusion.6), channel_id=7, replica_groups=mesh['dp'=8,'space'=32] {'space'}, dimensions={0}, use_global_device_ids=true | all-gather | bytes 33792 | tf_op jit(solution)/shard_map/all_gather | solution.py:57
  869.7 2.1 fusion.4
  873.8 2.8 collective-permute-start.4
  876.6 4.6 collective-permute-start.3
  881.1 4.0 collective-permute-start.2
  886.9 4.5 concatenate.99
  892.2 4.3 copy.88
  896.5 3.5 scatter_fusion.9
  900.0 2.5 convert_element_type.164
  902.5 2.5 copy.89
  905.0 30.0 %all-reduce.6.cloned.1.call-done = bf16[128,512]{1,0:T(8,128)(2,1)} async-done(((bf16[128,512]{1,0:T(8,128)(2,1)}), bf16[128,512]{1,0:T(8,128)(2,1)}) %all-reduce.6.cloned.1.call-update) | async-done | bytes 131088
  935.7 197.0 %reduce-scatter.9.cloned.1.call-done = bf16[16,128]{1,0:T(8,128)(2,1)} async-done(((bf16[512,128]{1,0:T(8,128)(2,1)}), bf16[16,128]{1,0:T(8,128)(2,1)}) %reduce-scatter.9.cloned.1.call-update) | async-done | bytes 4112
  1133.5 218.3 %reduce-scatter.11.cloned.1.call-done = bf16[16,512]{1,0:T(8,128)(2,1)} async-done(((bf16[512,512]{1,0:T(8,128)(2,1)}), bf16[16,512]{1,0:T(8,128)(2,1)}) %reduce-scatter.11.cloned.1.call-update) | async-done | bytes 16400
  1352.7 25.6 %all-reduce.3 = (bf16[16,128]{0,1:T(8,128)(2,1)S(1)}, bf16[36,128]{1,0:T(8,128)(2,1)S(1)}, bf16[4,512]{1,0:T(4,128)(2,1)S(1)}, bf16[16,512]{0,1:T(8,128)(2,1)S(1...) all-reduce(bf16[16,128]{0,1:T(8,128)(2,1)S(1)} %copy.93, ...), channel_id=1, replica_groups=mesh['dp'=8,'space'=32] {'dp'}, use_global_device_ids=true, to_apply=%region_49.50 | all-reduce | flops 19456 | bytes 77824 | tf_op jit(solution)/shard_map/psum | solution.py:272
  1382.9 2.6 reshape.382
  (382 shorter events, 68.5 us)
Async XLA Ops:
  7.2 289.5 %copy-start = (bf16[512,512]{1,0:T(8,128)(2,1)S(1)}, bf16[512,512]{1,0:T(8,128)(2,1)}, u32[]{:S(2)}) copy-start(bf16[512,512]{1,0:T(8,128)(2,1)} %param.25) | copy-start | bytes 1572868
  9.9 11.8 copy-start.10
  9.9 515.5 %all-to-all-start.1 = ((bf16[32,2,8192]{2,1,0:T(2,128)(2,1)}), bf16[32,2,8192]{2,1,0:T(2,128)(2,1)}, u32[]{:S(2)}, u32[]{:S(2)}) async-start(bf16[32,2,8192]{2,1,0:T(2,128)(2,1)} %reshape_squeeze.49), calls=%async_computation.1 | async-start | bytes 2097152 | tf_op jit(solution)/shard_map/all_to_all | solution.py:90
  21.7 913.3 %all-reduce.6.cloned.1.call-start = ((), (), s32[]{:S(2)}) async-start(), calls=%async_computation.6 | async-start | bytes 262144
  21.7 58.5 %copy-start.47 = (f32[2,128]{1,0:T(2,128)S(1)}, f32[2,128]{1,0:T(2,128)}, u32[]{:S(2)}) copy-start(f32[2,128]{1,0:T(2,128)} %param.26) | copy-start | bytes 3076
  21.7 58.5 %copy-start.60 = (f32[2,128]{1,0:T(2,128)S(1)}, f32[2,128]{1,0:T(2,128)}, u32[]{:S(2)}) copy-start(f32[2,128]{1,0:T(2,128)} %param.27) | copy-start | bytes 3076
  82.3 155.4 %copy-start.59 = (s32[1,32,3]{1,0,2:T(1,128)S(1)}, s32[1,32,3]{1,0,2:T(1,128)}, u32[]{:S(2)}) copy-start(s32[1,32,3]{1,0,2:T(1,128)} %param.21) | copy-start | bytes 1156
  82.3 156.5 %copy-start.46 = (f32[2,512]{1,0:T(2,128)S(1)}, f32[2,512]{1,0:T(2,128)}, u32[]{:S(2)}) copy-start(f32[2,512]{1,0:T(2,128)} %param.29) | copy-start | bytes 12292
  82.3 157.0 %copy-start.25 = (f32[2,512]{1,0:T(2,128)S(1)}, f32[2,512]{1,0:T(2,128)}, u32[]{:S(2)}) copy-start(f32[2,512]{1,0:T(2,128)} %param.28) | copy-start | bytes 12292
  82.3 163.4 %copy-start.51 = (s32[1,32,1]{1,2,0:T(1,128)S(1)}, s32[1,32,1]{1,2,0:T(1,128)}, u32[]{:S(2)}) copy-start(s32[1,32,1]{1,2,0:T(1,128)} %param.20) | copy-start | bytes 388
  83.2 215.9 %collective-permute-start = (bf16[32,2048]{1,0:T(8,128)(2,1)}, bf16[32,2048]{1,0:T(8,128)(2,1)S(1)}, u32[]{:S(2)}, u32[]{:S(2)}) collective-permute-start(bf16[32,2048]{1,0:T(8,128)(2,1)} %bitcast.220), channel_id=1, source_target_pairs={{0,1},{1,2},{2,3},{3,4},{4,5},{5,6},{6,7},{7,8},{8,9},{9,10},{10,1... | collective-permute-start | bytes 393224 | tf_op jit(solution)/shard_map/ppermute | solution.py:15
  294.0 5.2 copy-start.11
  294.0 4.6 copy-start.52
  294.0 4.6 copy-start.64
  412.8 13.2 copy-start.16
  412.8 13.9 copy-start.15
  412.8 15.3 %copy-start.14 = (bf16[32,4,4,128]{3,2,1,0:T(4,128)(2,1)S(1)}, bf16[32,4,4,128]{3,2,1,0:T(4,128)(2,1)}, u32[]{:S(2)}) copy-start(bf16[32,4,4,128]{3,2,1,0:T(4,128)(2,1)} %slice.295) | copy-start | bytes 393220
  412.8 16.0 %copy-start.13 = (bf16[32,4,4,128]{3,2,1,0:T(4,128)(2,1)S(1)}, bf16[32,4,4,128]{3,2,1,0:T(4,128)(2,1)}, u32[]{:S(2)}) copy-start(bf16[32,4,4,128]{3,2,1,0:T(4,128)(2,1)} %slice.296) | copy-start | bytes 393220
  431.9 42.3 %copy-start.57 = (f32[128]{0:T(128)S(1)}, f32[128]{0:T(128)}, u32[]{:S(2)}) copy-start(f32[128]{0:T(128)} %get-tuple-element.173) | copy-start | bytes 1540
  431.9 42.3 %copy-start.67 = (f32[128]{0:T(128)S(1)}, f32[128]{0:T(128)}, u32[]{:S(2)}) copy-start(f32[128]{0:T(128)} %get-tuple-element.163) | copy-start | bytes 1540
  432.4 91.4 %copy-start.8 = (f32[512,128]{1,0:T(8,128)}, f32[512,128]{1,0:T(8,128)S(1)}, u32[]{:S(2)}) copy-start(f32[512,128]{1,0:T(8,128)S(1)} %get-tuple-element.168) | copy-start | bytes 786436
  432.4 43.8 %copy-start.53 = (f32[512]{0:T(512)S(1)}, f32[512]{0:T(512)}, u32[]{:S(2)}) copy-start(f32[512]{0:T(512)} %get-tuple-element.83) | copy-start | bytes 6148
  432.4 43.8 %copy-start.54 = (f32[512]{0:T(512)S(1)}, f32[512]{0:T(512)}, u32[]{:S(2)}) copy-start(f32[512]{0:T(512)} %get-tuple-element.84) | copy-start | bytes 6148
  473.7 50.1 %copy-start.55 = (f32[128]{0:T(128)}, f32[128]{0:T(128)S(1)}, u32[]{:S(2)}) copy-start(f32[128]{0:T(128)S(1)} %div.98) | copy-start | bytes 1540
  474.1 49.7 %copy-start.69 = (f32[128]{0:T(128)}, f32[128]{0:T(128)S(1)}, u32[]{:S(2)}) copy-start(f32[128]{0:T(128)S(1)} %add_rsqrt_fusion.2) | copy-start | bytes 1540
  523.8 3.9 copy-start.50
  532.7 67.4 %copy-start.26 = (f32[2,512]{1,0:T(2,128)S(1)}, f32[2,512]{1,0:T(2,128)}, u32[]{:S(2)}) copy-start(f32[2,512]{1,0:T(2,128)} %param.28) | copy-start | bytes 12292
  600.1 4.5 copy-start.21
  601.6 3.8 copy-start.9
  601.6 3.8 copy-start.56
  601.6 3.8 copy-start.58
  601.6 3.8 copy-start.68
  606.4 43.6 %copy-start.48 = (f32[2,128]{1,0:T(2,128)S(1)}, f32[2,128]{1,0:T(2,128)}, u32[]{:S(2)}) copy-start(f32[2,128]{1,0:T(2,128)} %param.26) | copy-start | bytes 3076
  653.2 95.7 %copy-start.5 = (bf16[512,512]{1,0:T(8,128)(2,1)S(1)}, bf16[512,512]{1,0:T(8,128)(2,1)}, u32[]{:S(2)}) copy-start(bf16[512,512]{1,0:T(8,128)(2,1)} %get-tuple-element.128) | copy-start | bytes 1572868
  728.9 147.6 %collective-permute-start.8 = (bf16[48,128]{1,0:T(8,128)(2,1)}, bf16[48,128]{1,0:T(8,128)(2,1)}, u32[]{:S(2)}, u32[]{:S(2)}) collective-permute-start(bf16[48,128]{1,0:T(8,128)(2,1)} %fusion), channel_id=1, source_target_pairs={{0,7},{1,8},{2,9},{3,10},{4,11},{5,12},{6,13},{7,14},{8,15},{9,16}... | collective-permute-start | bytes 36872
  730.8 150.3 %collective-permute-start.7 = (bf16[48,128]{1,0:T(8,128)(2,1)}, bf16[48,128]{1,0:T(8,128)(2,1)}, u32[]{:S(2)}, u32[]{:S(2)}) collective-permute-start(bf16[48,128]{1,0:T(8,128)(2,1)} %fusion), channel_id=1, source_target_pairs={{0,6},{1,7},{2,8},{3,9},{4,10},{5,11},{6,12},{7,13},{8,14},{9,15},... | collective-permute-start | bytes 36872
  739.8 146.2 %collective-permute-start.6 = (bf16[48,128]{1,0:T(8,128)(2,1)}, bf16[48,128]{1,0:T(8,128)(2,1)}, u32[]{:S(2)}, u32[]{:S(2)}) collective-permute-start(bf16[48,128]{1,0:T(8,128)(2,1)} %fusion), channel_id=1, source_target_pairs={{0,5},{1,6},{2,7},{3,8},{4,9},{5,10},{6,11},{7,12},{8,13},{9,14},{... | collective-permute-start | bytes 36872
  741.7 144.4 %collective-permute-start.5 = (bf16[48,128]{1,0:T(8,128)(2,1)}, bf16[48,128]{1,0:T(8,128)(2,1)}, u32[]{:S(2)}, u32[]{:S(2)}) collective-permute-start(bf16[48,128]{1,0:T(8,128)(2,1)} %fusion), channel_id=1, source_target_pairs={{0,4},{1,5},{2,6},{3,7},{4,8},{5,9},{6,10},{7,11},{8,12},{9,13},{1... | collective-permute-start | bytes 36872
  797.8 7.5 copy-start.18
  797.8 7.6 copy-start.39
  797.8 7.6 copy-start.43
  797.8 8.0 copy-start.17
  797.8 8.1 copy-start.37
  797.8 8.1 copy-start.41
  797.8 8.5 copy-start.63
  797.8 8.5 copy-start.66
  797.8 585.1 %all-to-all-start = ((bf16[32,2,8192]{2,1,0:T(2,128)(2,1)}), bf16[32,2,8192]{2,1,0:T(2,128)(2,1)}, u32[]{:S(2)}, u32[]{:S(2)}) async-start(bf16[32,2,8192]{2,1,0:T(2,128)(2,1)} %reshape.381), calls=%async_computation | async-start | bytes 2097152 | tf_op jit(solution)/shard_map/all_to_all | solution.py:193
  805.0 4.2 copy-start.22
  805.0 9.0 copy-start.27
  805.0 327.7 %reduce-scatter.9.cloned.1.call-start = ((), (), s32[]{:S(2)}) async-start(), calls=%async_computation.4 | async-start | bytes 135168
  806.6 11.9 copy-start.2
  806.6 7.4 collective-permute-start.1
  809.2 9.3 copy-start.3
  814.0 59.8 %collective-permute-start.9 = (bf16[36,128]{1,0:T(8,128)(2,1)S(1)}, bf16[36,128]{1,0:T(8,128)(2,1)S(1)}, u32[]{:S(2)}, u32[]{:S(2)}) collective-permute-start(bf16[36,128]{1,0:T(8,128)(2,1)S(1)} %copy-done.27), channel_id=1, source_target_pairs={{0,8},{1,9},{2,10},{3,11},{4,12},{5,13},{6,14},{7,15},{8,16},{9,17... | collective-permute-start | bytes 27656
  819.9 48.6 %copy-start.49 = (f32[2,128]{1,0:T(2,128)S(1)}, f32[2,128]{1,0:T(2,128)}, u32[]{:S(2)}) copy-start(f32[2,128]{1,0:T(2,128)} %param.26) | copy-start | bytes 3076
  819.9 49.5 %copy-start.45 = (f32[128]{0:T(128)S(1)}, f32[128]{0:T(128)}, u32[]{:S(2)}) copy-start(f32[128]{0:T(128)} %copy-done.44) | copy-start | bytes 1540
  871.8 13.3 copy-start.4
  872.6 479.3 %reduce-scatter.11.cloned.1.call-start = ((), (), s32[]{:S(2)}) async-start(), calls=%async_computation.5 | async-start | bytes 540672
  873.8 12.3 collective-permute-start.4
  876.6 9.6 collective-permute-start.3
  881.1 5.8 collective-permute-start.2
  892.2 4.3 copy-start.20
  902.5 478.6 %copy-start.61 = (f32[2]{0:T(128)S(1)}, f32[2]{0:T(128)}, u32[]{:S(2)}) copy-start(f32[2]{0:T(128)} %constant.157) | copy-start | bytes 28
  1379.1 6.4 copy-start.1
  (22 other events, 48.9 us)
Sparse Core Ops, SparseCore 0:
  793.1 141.8 all-reduce.5
  938.7 194.0 reduce-scatter.8
  1137.1 214.7 reduce-scatter.10
